TPU v7x, 256 devices: a whole 4x4x8 slice. The times are simulated.
256 devices in a mesh: section: 2 (over x_lo), ctx: 128 (over z, y, x_hi, core).
Axes of the slice: x: 4 (x_hi: 2, x_lo: 2; x = x_hi * 2 + x_lo), y: 4, z: 8, core: 2. Of those that a mesh axis runs over, the one named last changes fastest.
Arguments:
- stream: bfloat16 [2, 24576, 8192], P('section', 'ctx'), may hold values from -1.5 to 1.5
- queries: bfloat16 [2, 24576, 8192], P('section', 'ctx'), may hold values from -24 to 24
- keys: bfloat16 [2, 24576, 1024], P('section', 'ctx'), may hold values from -24 to 24
- values: bfloat16 [2, 24576, 1024], P('section', 'ctx'), may hold values from -6 to 6
- segments: int32 [2, 24576], P('section', 'ctx'), may hold values from 0 to 63, never falling along the last dimension, each value on 1 to 1344 neighbouring positions
Outputs:
- next_stream: bfloat16 [2, 24576, 8192], P('section', 'ctx')
Inputs may be any that keep to these rules, and one draw needn't show every extreme that they name: `segments`: along each micro-batch the numbers never fall; each document holds at most (7) * 192 tokens, and one holds exactly that many.
All inputs are finite; a program needn't handle non-finite values.
Results may differ from a plain program's by a relative error of at most 0.0095.
Values may be sent and summed in bfloat16 or wider, within the bound.
A program may use at most 128 MiB of HBM per device.

v0:
```python
import jax
import jax.numpy as jnp
from jax import lax
from jax.sharding import PartitionSpec as P

HQ = 64
KVH = 8
HD = 128
WINDOW = 8


def shifted(value, axis, by):
    size = lax.axis_size(axis)
    pairs = [(i, i + by) for i in range(size) if 0 <= i + by < size]
    return lax.ppermute(value, axis, pairs)


def from_behind(value, axis, by):
    size = lax.axis_size(axis)
    return lax.ppermute(value, axis, [(i, (i + by) % size) for i in range(size)])


def attend_window(query_rows, key_rows, value_rows, seg_query, seg_key, pos_query, pos_key):
    tok_count = query_rows.shape[0]
    key_count = key_rows.shape[0]
    repeat = HQ // KVH
    query_groups = jnp.moveaxis(query_rows.reshape(tok_count, KVH, repeat, HD), 1, 0)
    key_groups = jnp.moveaxis(key_rows.reshape(key_count, KVH, HD), 1, 0)
    value_groups = jnp.moveaxis(value_rows.reshape(key_count, KVH, HD), 1, 0)
    visible = (
        (seg_query[:, None] == seg_key[None, :])
        & (pos_key[None, :] <= pos_query[:, None])
        & (pos_key[None, :] >= 0)
    )

    def one_group(group_parts):
        query_group, key_group, value_group = group_parts
        scores = jnp.einsum(
            "trd,ld->rtl", query_group, key_group, preferred_element_type=jnp.float32
        ) * HD ** (-0.5)
        scores = jnp.where(visible[None, :, :], scores, jnp.float32(-1e30))
        top_score = jnp.max(scores, axis=-1, keepdims=True)
        expo = jnp.exp(scores - top_score)
        probs = (expo / jnp.sum(expo, axis=-1, keepdims=True)).astype(jnp.bfloat16)
        return jnp.einsum("rtl,ld->trd", probs, value_group, preferred_element_type=jnp.float32)

    group_out = lax.map(one_group, (query_groups, key_groups, value_groups))
    return jnp.moveaxis(group_out, 0, 1).reshape(tok_count, HQ * HD)


def local(stream, queries, keys, values, segments):
    tok_rows = queries.shape[1]
    kv_width = keys.shape[2]
    ctx_index = lax.axis_index("ctx")
    own_pair = jnp.concatenate([keys[0], values[0]], axis=1)
    own_seg = segments[0]
    pair_list = [own_pair]
    seg_list = [own_seg]
    moving = (own_pair, own_seg)
    for back_step in range(WINDOW - 1):
        moving = shifted((moving[0], moving[1]), "ctx", 1)
        pair_list.insert(0, moving[0])
        seg_list.insert(0, moving[1])
    window_pair = jnp.concatenate(pair_list, axis=0)
    window_seg = jnp.concatenate(seg_list, axis=0)
    window_keys = window_pair[:, :kv_width]
    window_values = window_pair[:, kv_width:]
    pos_query = ctx_index * tok_rows + jnp.arange(tok_rows, dtype=jnp.int32)
    pos_key = (ctx_index - (WINDOW - 1)) * tok_rows + jnp.arange(WINDOW * tok_rows, dtype=jnp.int32)
    query_rows = queries[0]
    attended = attend_window(
        query_rows, window_keys, window_values, own_seg, window_seg, pos_query, pos_key
    )
    updated = (stream[0].astype(jnp.float32) + attended).astype(jnp.bfloat16)
    return from_behind(updated[None], "section", 1)


def solution(mesh):
    in_specs = (
        P("section", "ctx", None),
        P("section", "ctx", None),
        P("section", "ctx", None),
        P("section", "ctx", None),
        P("section", "ctx"),
    )
    out_specs = P("section", "ctx", None)
    return jax.shard_map(local, mesh=mesh, in_specs=in_specs, out_specs=out_specs, check_vma=False)
```

profile of v0, /device:TPU:127, one launch (start us, length us, event | category | flops | bytes accessed | tf_op | source)
XLA Modules:
  0.0 442.4 jit_solution(8905669833128690700)
XLA Ops:
  8.9 8.9 %collective-permute-done = bf16[192,2048]{1,0:T(8,128)(2,1)S(1)} collective-permute-done((bf16[192,2048]{1,0:T(8,128)(2,1)S(1)}, bf16[192,2048]{1,0:T(8,128)(2,1)S(1)}, u32[]{:S(2)}, u32[]{:S(2)}) %collective-permute-start) | collective-permute-done | bytes 786464 | tf_op jit(solution)/shard_map/ppermute | solution.py:15
  17.9 10.1 %collective-permute-start.1 = (bf16[192,2048]{1,0:T(8,128)(2,1)S(1)}, bf16[192,2048]{1,0:T(8,128)(2,1)S(1)}, u32[]{:S(2)}, u32[]{:S(2)}) collective-permute-start(bf16[192,2048]{1,0:T(8,128)(2,1)S(1)} %collective-permute-done), channel_id=1, source_target_pairs={{0,1},{1,2},{2,3},{3,4},{4,5},{5,6},{6,7},{7,8},{8,9},{9,10},{10,1... | collective-permute-start | bytes 2359304 | tf_op jit(solution)/shard_map/ppermute | solution.py:15
  28.0 8.9 %collective-permute-done.1 = bf16[192,2048]{1,0:T(8,128)(2,1)S(1)} collective-permute-done((bf16[192,2048]{1,0:T(8,128)(2,1)S(1)}, bf16[192,2048]{1,0:T(8,128)(2,1)S(1)}, u32[]{:S(2)}, u32[]{:S(2)}) %collective-permute-start.1) | collective-permute-done | bytes 786464 | tf_op jit(solution)/shard_map/ppermute | solution.py:15
  36.9 10.1 %collective-permute-start.2 = (bf16[192,2048]{1,0:T(8,128)(2,1)S(1)}, bf16[192,2048]{1,0:T(8,128)(2,1)S(1)}, u32[]{:S(2)}, u32[]{:S(2)}) collective-permute-start(bf16[192,2048]{1,0:T(8,128)(2,1)S(1)} %collective-permute-done.1), channel_id=1, source_target_pairs={{0,1},{1,2},{2,3},{3,4},{4,5},{5,6},{6,7},{7,8},{8,9},{9,10},{10,1... | collective-permute-start | bytes 2359304 | tf_op jit(solution)/shard_map/ppermute | solution.py:15
  47.0 8.9 %collective-permute-done.2 = bf16[192,2048]{1,0:T(8,128)(2,1)S(1)} collective-permute-done((bf16[192,2048]{1,0:T(8,128)(2,1)S(1)}, bf16[192,2048]{1,0:T(8,128)(2,1)S(1)}, u32[]{:S(2)}, u32[]{:S(2)}) %collective-permute-start.2) | collective-permute-done | bytes 786464 | tf_op jit(solution)/shard_map/ppermute | solution.py:15
  56.8 10.1 %collective-permute-start.3 = (bf16[192,2048]{1,0:T(8,128)(2,1)S(1)}, bf16[192,2048]{1,0:T(8,128)(2,1)S(1)}, u32[]{:S(2)}, u32[]{:S(2)}) collective-permute-start(bf16[192,2048]{1,0:T(8,128)(2,1)S(1)} %collective-permute-done.2), channel_id=1, source_target_pairs={{0,1},{1,2},{2,3},{3,4},{4,5},{5,6},{6,7},{7,8},{8,9},{9,10},{10,1... | collective-permute-start | bytes 2359304 | tf_op jit(solution)/shard_map/ppermute | solution.py:15
  66.9 8.9 %collective-permute-done.3 = bf16[192,2048]{1,0:T(8,128)(2,1)S(1)} collective-permute-done((bf16[192,2048]{1,0:T(8,128)(2,1)S(1)}, bf16[192,2048]{1,0:T(8,128)(2,1)S(1)}, u32[]{:S(2)}, u32[]{:S(2)}) %collective-permute-start.3) | collective-permute-done | bytes 786464 | tf_op jit(solution)/shard_map/ppermute | solution.py:15
  76.8 10.1 %collective-permute-start.4 = (bf16[192,2048]{1,0:T(8,128)(2,1)S(1)}, bf16[192,2048]{1,0:T(8,128)(2,1)S(1)}, u32[]{:S(2)}, u32[]{:S(2)}) collective-permute-start(bf16[192,2048]{1,0:T(8,128)(2,1)S(1)} %collective-permute-done.3), channel_id=1, source_target_pairs={{0,1},{1,2},{2,3},{3,4},{4,5},{5,6},{6,7},{7,8},{8,9},{9,10},{10,1... | collective-permute-start | bytes 2359304 | tf_op jit(solution)/shard_map/ppermute | solution.py:15
  86.9 8.9 %collective-permute-done.4 = bf16[192,2048]{1,0:T(8,128)(2,1)S(1)} collective-permute-done((bf16[192,2048]{1,0:T(8,128)(2,1)S(1)}, bf16[192,2048]{1,0:T(8,128)(2,1)S(1)}, u32[]{:S(2)}, u32[]{:S(2)}) %collective-permute-start.4) | collective-permute-done | bytes 786464 | tf_op jit(solution)/shard_map/ppermute | solution.py:15
  96.7 10.1 %collective-permute-start.5 = (bf16[192,2048]{1,0:T(8,128)(2,1)S(1)}, bf16[192,2048]{1,0:T(8,128)(2,1)}, u32[]{:S(2)}, u32[]{:S(2)}) collective-permute-start(bf16[192,2048]{1,0:T(8,128)(2,1)S(1)} %collective-permute-done.4), channel_id=1, source_target_pairs={{0,1},{1,2},{2,3},{3,4},{4,5},{5,6},{6,7},{7,8},{8,9},{9,10},{10,1... | collective-permute-start | bytes 2359304 | tf_op jit(solution)/shard_map/ppermute | solution.py:15
  106.8 8.9 %collective-permute-done.5 = bf16[192,2048]{1,0:T(8,128)(2,1)} collective-permute-done((bf16[192,2048]{1,0:T(8,128)(2,1)S(1)}, bf16[192,2048]{1,0:T(8,128)(2,1)}, u32[]{:S(2)}, u32[]{:S(2)}) %collective-permute-start.5) | collective-permute-done | bytes 786464 | tf_op jit(solution)/shard_map/ppermute | solution.py:15
  115.7 10.2 %collective-permute-start.6 = (bf16[192,2048]{1,0:T(8,128)(2,1)}, bf16[192,2048]{1,0:T(8,128)(2,1)}, u32[]{:S(2)}, u32[]{:S(2)}) collective-permute-start(bf16[192,2048]{1,0:T(8,128)(2,1)} %collective-permute-done.5), channel_id=1, source_target_pairs={{0,1},{1,2},{2,3},{3,4},{4,5},{5,6},{6,7},{7,8},{8,9},{9,10},{10,1... | collective-permute-start | bytes 2359304 | tf_op jit(solution)/shard_map/ppermute | solution.py:15
  127.9 7.3 %collective-permute-done.7 = s32[192]{0:T(256)S(1)} collective-permute-done((s32[192]{0:T(256)}, s32[192]{0:T(256)S(1)}, u32[]{:S(2)}, u32[]{:S(2)}) %collective-permute-start.7) | collective-permute-done | bytes 800 | tf_op jit(solution)/shard_map/ppermute | solution.py:15
  135.2 10.1 %collective-permute-start.8 = (s32[192]{0:T(256)S(1)}, s32[192]{0:T(256)S(1)}, u32[]{:S(2)}, u32[]{:S(2)}) collective-permute-start(s32[192]{0:T(256)S(1)} %collective-permute-done.7), channel_id=1, source_target_pairs={{0,1},{1,2},{2,3},{3,4},{4,5},{5,6},{6,7},{7,8},{8,9},{9,10},{10,1... | collective-permute-start | bytes 2312 | tf_op jit(solution)/shard_map/ppermute | solution.py:15
  146.0 9.9 %collective-permute-start.9 = (s32[192]{0:T(256)S(1)}, s32[192]{0:T(256)S(1)}, u32[]{:S(2)}, u32[]{:S(2)}) collective-permute-start(s32[192]{0:T(256)S(1)} %collective-permute-done.8), channel_id=1, source_target_pairs={{0,1},{1,2},{2,3},{3,4},{4,5},{5,6},{6,7},{7,8},{8,9},{9,10},{10,1... | collective-permute-start | bytes 2312 | tf_op jit(solution)/shard_map/ppermute | solution.py:15
  156.6 9.9 %collective-permute-start.10 = (s32[192]{0:T(256)S(1)}, s32[192]{0:T(256)S(1)}, u32[]{:S(2)}, u32[]{:S(2)}) collective-permute-start(s32[192]{0:T(256)S(1)} %collective-permute-done.9), channel_id=1, source_target_pairs={{0,1},{1,2},{2,3},{3,4},{4,5},{5,6},{6,7},{7,8},{8,9},{9,10},{10,1... | collective-permute-start | bytes 2312 | tf_op jit(solution)/shard_map/ppermute | solution.py:15
  167.2 9.9 %collective-permute-start.11 = (s32[192]{0:T(256)S(1)}, s32[192]{0:T(256)S(1)}, u32[]{:S(2)}, u32[]{:S(2)}) collective-permute-start(s32[192]{0:T(256)S(1)} %collective-permute-done.10), channel_id=1, source_target_pairs={{0,1},{1,2},{2,3},{3,4},{4,5},{5,6},{6,7},{7,8},{8,9},{9,10},{10,1... | collective-permute-start | bytes 2312 | tf_op jit(solution)/shard_map/ppermute | solution.py:15
  177.8 9.9 %collective-permute-start.12 = (s32[192]{0:T(256)S(1)}, s32[192]{0:T(256)S(1)}, u32[]{:S(2)}, u32[]{:S(2)}) collective-permute-start(s32[192]{0:T(256)S(1)} %collective-permute-done.11), channel_id=1, source_target_pairs={{0,1},{1,2},{2,3},{3,4},{4,5},{5,6},{6,7},{7,8},{8,9},{9,10},{10,1... | collective-permute-start | bytes 2312 | tf_op jit(solution)/shard_map/ppermute | solution.py:15
  188.4 9.9 %collective-permute-start.13 = (s32[192]{0:T(256)S(1)}, s32[192]{0:T(256)S(1)}, u32[]{:S(2)}, u32[]{:S(2)}) collective-permute-start(s32[192]{0:T(256)S(1)} %collective-permute-done.12), channel_id=1, source_target_pairs={{0,1},{1,2},{2,3},{3,4},{4,5},{5,6},{6,7},{7,8},{8,9},{9,10},{10,1... | collective-permute-start | bytes 2312 | tf_op jit(solution)/shard_map/ppermute | solution.py:15
  216.1 11.8 %concatenate.10 = bf16[1536,2048]{0,1:T(8,128)(2,1)} concatenate(bf16[192,2048]{0,1:T(8,128)(2,1)} %copy.16, bf16[192,2048]{0,1:T(8,128)(2,1)} %copy.17, bf16[192,2048]{0,1:T(8,128)(2,1)} %copy.18, bf16[192,2048]{0,1:T(8,128)(2,1)} %copy.19, bf16[192,2048]{0,1:T(8,128)(2,1)} %copy.20, bf16[192,2048]{0,1:T(8,128)(2,1)S(1)} %copy.21, bf16[192,2048]{0,1:T(8,128)(2,1)S(1)} %copy.22, ...), dimensions={0} | concatenate | bytes 12582912 | tf_op jit(solution)/shard_map/concatenate | solution.py:64
  233.8 124.1 %while.11 = (s32[]{:T(128)}, f32[8,192,8,128]{3,1,2,0:T(8,128)}, bf16[8,1536,128]{1,2,0:T(8,128)(2,1)}, bf16[8,1536,128]{1,2,0:T(8,128)(2,1)}, bf16[8,192,8,128]...) while((s32[]{:T(128)}, f32[8,192,8,128]{3,1,2,0:T(8,128)}, ...), condition=%wide.region_3.4_spmd.clone, body=%wide.region_0.3_spmd.clone.sunk | while | flops 1223296512 | bytes 22246000 | solution.py:47
  235.2 8.0 %fusion.44 = (f32[8,192]{1,0:T(8,128)S(1)}, f32[8,192,1536]{2,1,0:T(8,128)}) fusion(pred[192,1536]{1,0:T(8,128)(4,1)S(1)} %and_and_fusion.2, bf16[1,192,8,128]{3,2,0,1:T(8,128)(2,1)S(1)} %constant_dynamic-slice_fusion.2, bf16[8,1536,128]{1,2,0:T(8,128)(2,1)} %get-tuple-element.199, s32[]{:T(128)} %get-tuple-element.185), kind=kOutput, calls=%fused_computation.33.clone.1 | convolution fusion | flops 613418496 | bytes 10525184 | tf_op jit(solution)/shard_map/while/body/eval_jaxpr/sub | solution.py:43
  250.7 8.0 %fusion.44 = (f32[8,192]{1,0:T(8,128)S(1)}, f32[8,192,1536]{2,1,0:T(8,128)}) fusion(pred[192,1536]{1,0:T(8,128)(4,1)S(1)} %and_and_fusion.2, bf16[1,192,8,128]{3,2,0,1:T(8,128)(2,1)S(1)} %constant_dynamic-slice_fusion.2, bf16[8,1536,128]{1,2,0:T(8,128)(2,1)} %get-tuple-element.199, s32[]{:T(128)} %get-tuple-element.185), kind=kOutput, calls=%fused_computation.33.clone.1 | convolution fusion | flops 613418496 | bytes 10525184 | tf_op jit(solution)/shard_map/while/body/eval_jaxpr/sub | solution.py:43
  266.2 8.0 %fusion.44 = (f32[8,192]{1,0:T(8,128)S(1)}, f32[8,192,1536]{2,1,0:T(8,128)}) fusion(pred[192,1536]{1,0:T(8,128)(4,1)S(1)} %and_and_fusion.2, bf16[1,192,8,128]{3,2,0,1:T(8,128)(2,1)S(1)} %constant_dynamic-slice_fusion.2, bf16[8,1536,128]{1,2,0:T(8,128)(2,1)} %get-tuple-element.199, s32[]{:T(128)} %get-tuple-element.185), kind=kOutput, calls=%fused_computation.33.clone.1 | convolution fusion | flops 613418496 | bytes 10525184 | tf_op jit(solution)/shard_map/while/body/eval_jaxpr/sub | solution.py:43
  281.7 8.0 %fusion.44 = (f32[8,192]{1,0:T(8,128)S(1)}, f32[8,192,1536]{2,1,0:T(8,128)}) fusion(pred[192,1536]{1,0:T(8,128)(4,1)S(1)} %and_and_fusion.2, bf16[1,192,8,128]{3,2,0,1:T(8,128)(2,1)S(1)} %constant_dynamic-slice_fusion.2, bf16[8,1536,128]{1,2,0:T(8,128)(2,1)} %get-tuple-element.199, s32[]{:T(128)} %get-tuple-element.185), kind=kOutput, calls=%fused_computation.33.clone.1 | convolution fusion | flops 613418496 | bytes 10525184 | tf_op jit(solution)/shard_map/while/body/eval_jaxpr/sub | solution.py:43
  297.2 8.0 %fusion.44 = (f32[8,192]{1,0:T(8,128)S(1)}, f32[8,192,1536]{2,1,0:T(8,128)}) fusion(pred[192,1536]{1,0:T(8,128)(4,1)S(1)} %and_and_fusion.2, bf16[1,192,8,128]{3,2,0,1:T(8,128)(2,1)S(1)} %constant_dynamic-slice_fusion.2, bf16[8,1536,128]{1,2,0:T(8,128)(2,1)} %get-tuple-element.199, s32[]{:T(128)} %get-tuple-element.185), kind=kOutput, calls=%fused_computation.33.clone.1 | convolution fusion | flops 613418496 | bytes 10525184 | tf_op jit(solution)/shard_map/while/body/eval_jaxpr/sub | solution.py:43
  312.8 8.0 %fusion.44 = (f32[8,192]{1,0:T(8,128)S(1)}, f32[8,192,1536]{2,1,0:T(8,128)}) fusion(pred[192,1536]{1,0:T(8,128)(4,1)S(1)} %and_and_fusion.2, bf16[1,192,8,128]{3,2,0,1:T(8,128)(2,1)S(1)} %constant_dynamic-slice_fusion.2, bf16[8,1536,128]{1,2,0:T(8,128)(2,1)} %get-tuple-element.199, s32[]{:T(128)} %get-tuple-element.185), kind=kOutput, calls=%fused_computation.33.clone.1 | convolution fusion | flops 613418496 | bytes 10525184 | tf_op jit(solution)/shard_map/while/body/eval_jaxpr/sub | solution.py:43
  328.3 8.0 %fusion.44 = (f32[8,192]{1,0:T(8,128)S(1)}, f32[8,192,1536]{2,1,0:T(8,128)}) fusion(pred[192,1536]{1,0:T(8,128)(4,1)S(1)} %and_and_fusion.2, bf16[1,192,8,128]{3,2,0,1:T(8,128)(2,1)S(1)} %constant_dynamic-slice_fusion.2, bf16[8,1536,128]{1,2,0:T(8,128)(2,1)} %get-tuple-element.199, s32[]{:T(128)} %get-tuple-element.185), kind=kOutput, calls=%fused_computation.33.clone.1 | convolution fusion | flops 613418496 | bytes 10525184 | tf_op jit(solution)/shard_map/while/body/eval_jaxpr/sub | solution.py:43
  343.8 8.0 %fusion.44 = (f32[8,192]{1,0:T(8,128)S(1)}, f32[8,192,1536]{2,1,0:T(8,128)}) fusion(pred[192,1536]{1,0:T(8,128)(4,1)S(1)} %and_and_fusion.2, bf16[1,192,8,128]{3,2,0,1:T(8,128)(2,1)S(1)} %constant_dynamic-slice_fusion.2, bf16[8,1536,128]{1,2,0:T(8,128)(2,1)} %get-tuple-element.199, s32[]{:T(128)} %get-tuple-element.185), kind=kOutput, calls=%fused_computation.33.clone.1 | convolution fusion | flops 613418496 | bytes 10525184 | tf_op jit(solution)/shard_map/while/body/eval_jaxpr/sub | solution.py:43
  357.9 9.1 %copy.26 = f32[192,8,8,128]{3,2,1,0:T(8,128)} copy(f32[192,8,8,128]{3,0,2,1:T(8,128)} %bitcast.76) | data formatting | bytes 12582912 | tf_op jit(solution)/shard_map/transpose | solution.py:48
  367.0 7.3 %reshape.29 = f32[1,192,8192]{2,1,0:T(8,128)} reshape(f32[192,8,8,128]{3,2,1,0:T(8,128)} %copy.26) | data formatting | bytes 12582912 | tf_op jit(solution)/shard_map/reshape | solution.py:48
  377.9 62.8 %collective-permute-done.14 = bf16[1,192,8192]{2,1,0:T(8,128)(2,1)S(1)} collective-permute-done((bf16[1,192,8192]{2,1,0:T(8,128)(2,1)S(1)}, bf16[1,192,8192]{2,1,0:T(8,128)(2,1)S(1)}, u32[]{:S(2)}, u32[]{:S(2)}) %collective-permute-start.14) | collective-permute-done | bytes 3145760 | tf_op jit(solution)/shard_map/ppermute | solution.py:20
  (66 shorter events, 106.5 us)
Async XLA Ops:
  0.0 202.7 %copy-start.5 = (s32[1,192]{1,0:T(1,128)S(1)}, s32[1,192]{1,0:T(1,128)}, u32[]{:S(2)}) copy-start(s32[1,192]{1,0:T(1,128)} %param.11) | copy-start | bytes 2308
  3.1 14.7 %collective-permute-start = (bf16[192,2048]{1,0:T(8,128)(2,1)S(1)}, bf16[192,2048]{1,0:T(8,128)(2,1)S(1)}, u32[]{:S(2)}, u32[]{:S(2)}) collective-permute-start(bf16[192,2048]{1,0:T(8,128)(2,1)S(1)} %copy.15), channel_id=1, source_target_pairs={{0,1},{1,2},{2,3},{3,4},{4,5},{5,6},{6,7},{7,8},{8,9},{9,10},{10,1... | collective-permute-start | bytes 2359304 | tf_op jit(solution)/shard_map/ppermute | solution.py:15
  17.9 19.0 %collective-permute-start.1 = (bf16[192,2048]{1,0:T(8,128)(2,1)S(1)}, bf16[192,2048]{1,0:T(8,128)(2,1)S(1)}, u32[]{:S(2)}, u32[]{:S(2)}) collective-permute-start(bf16[192,2048]{1,0:T(8,128)(2,1)S(1)} %collective-permute-done), channel_id=1, source_target_pairs={{0,1},{1,2},{2,3},{3,4},{4,5},{5,6},{6,7},{7,8},{8,9},{9,10},{10,1... | collective-permute-start | bytes 2359304 | tf_op jit(solution)/shard_map/ppermute | solution.py:15
  36.9 165.9 %copy-start.1 = (bf16[192,2048]{1,0:T(8,128)(2,1)}, bf16[192,2048]{1,0:T(8,128)(2,1)S(1)}, u32[]{:S(2)}) copy-start(bf16[192,2048]{1,0:T(8,128)(2,1)S(1)} %collective-permute-done.1) | copy-start | bytes 2359300
  36.9 19.0 %collective-permute-start.2 = (bf16[192,2048]{1,0:T(8,128)(2,1)S(1)}, bf16[192,2048]{1,0:T(8,128)(2,1)S(1)}, u32[]{:S(2)}, u32[]{:S(2)}) collective-permute-start(bf16[192,2048]{1,0:T(8,128)(2,1)S(1)} %collective-permute-done.1), channel_id=1, source_target_pairs={{0,1},{1,2},{2,3},{3,4},{4,5},{5,6},{6,7},{7,8},{8,9},{9,10},{10,1... | collective-permute-start | bytes 2359304 | tf_op jit(solution)/shard_map/ppermute | solution.py:15
  55.9 0.9 copy-start.2
  56.8 19.0 %collective-permute-start.3 = (bf16[192,2048]{1,0:T(8,128)(2,1)S(1)}, bf16[192,2048]{1,0:T(8,128)(2,1)S(1)}, u32[]{:S(2)}, u32[]{:S(2)}) collective-permute-start(bf16[192,2048]{1,0:T(8,128)(2,1)S(1)} %collective-permute-done.2), channel_id=1, source_target_pairs={{0,1},{1,2},{2,3},{3,4},{4,5},{5,6},{6,7},{7,8},{8,9},{9,10},{10,1... | collective-permute-start | bytes 2359304 | tf_op jit(solution)/shard_map/ppermute | solution.py:15
  75.8 1.0 copy-start.3
  76.8 19.0 %collective-permute-start.4 = (bf16[192,2048]{1,0:T(8,128)(2,1)S(1)}, bf16[192,2048]{1,0:T(8,128)(2,1)S(1)}, u32[]{:S(2)}, u32[]{:S(2)}) collective-permute-start(bf16[192,2048]{1,0:T(8,128)(2,1)S(1)} %collective-permute-done.3), channel_id=1, source_target_pairs={{0,1},{1,2},{2,3},{3,4},{4,5},{5,6},{6,7},{7,8},{8,9},{9,10},{10,1... | collective-permute-start | bytes 2359304 | tf_op jit(solution)/shard_map/ppermute | solution.py:15
  95.8 0.9 copy-start.4
  96.7 19.0 %collective-permute-start.5 = (bf16[192,2048]{1,0:T(8,128)(2,1)S(1)}, bf16[192,2048]{1,0:T(8,128)(2,1)}, u32[]{:S(2)}, u32[]{:S(2)}) collective-permute-start(bf16[192,2048]{1,0:T(8,128)(2,1)S(1)} %collective-permute-done.4), channel_id=1, source_target_pairs={{0,1},{1,2},{2,3},{3,4},{4,5},{5,6},{6,7},{7,8},{8,9},{9,10},{10,1... | collective-permute-start | bytes 2359304 | tf_op jit(solution)/shard_map/ppermute | solution.py:15
  115.7 98.1 %collective-permute-start.6 = (bf16[192,2048]{1,0:T(8,128)(2,1)}, bf16[192,2048]{1,0:T(8,128)(2,1)}, u32[]{:S(2)}, u32[]{:S(2)}) collective-permute-start(bf16[192,2048]{1,0:T(8,128)(2,1)} %collective-permute-done.5), channel_id=1, source_target_pairs={{0,1},{1,2},{2,3},{3,4},{4,5},{5,6},{6,7},{7,8},{8,9},{9,10},{10,1... | collective-permute-start | bytes 2359304 | tf_op jit(solution)/shard_map/ppermute | solution.py:15
  125.9 9.2 %collective-permute-start.7 = (s32[192]{0:T(256)}, s32[192]{0:T(256)S(1)}, u32[]{:S(2)}, u32[]{:S(2)}) collective-permute-start(s32[192]{0:T(256)} %bitcast.82), channel_id=1, source_target_pairs={{0,1},{1,2},{2,3},{3,4},{4,5},{5,6},{6,7},{7,8},{8,9},{9,10},{10,1... | collective-permute-start | bytes 2312 | tf_op jit(solution)/shard_map/ppermute | solution.py:15
  135.2 10.8 %collective-permute-start.8 = (s32[192]{0:T(256)S(1)}, s32[192]{0:T(256)S(1)}, u32[]{:S(2)}, u32[]{:S(2)}) collective-permute-start(s32[192]{0:T(256)S(1)} %collective-permute-done.7), channel_id=1, source_target_pairs={{0,1},{1,2},{2,3},{3,4},{4,5},{5,6},{6,7},{7,8},{8,9},{9,10},{10,1... | collective-permute-start | bytes 2312 | tf_op jit(solution)/shard_map/ppermute | solution.py:15
  146.0 10.6 %collective-permute-start.9 = (s32[192]{0:T(256)S(1)}, s32[192]{0:T(256)S(1)}, u32[]{:S(2)}, u32[]{:S(2)}) collective-permute-start(s32[192]{0:T(256)S(1)} %collective-permute-done.8), channel_id=1, source_target_pairs={{0,1},{1,2},{2,3},{3,4},{4,5},{5,6},{6,7},{7,8},{8,9},{9,10},{10,1... | collective-permute-start | bytes 2312 | tf_op jit(solution)/shard_map/ppermute | solution.py:15
  156.6 10.6 %collective-permute-start.10 = (s32[192]{0:T(256)S(1)}, s32[192]{0:T(256)S(1)}, u32[]{:S(2)}, u32[]{:S(2)}) collective-permute-start(s32[192]{0:T(256)S(1)} %collective-permute-done.9), channel_id=1, source_target_pairs={{0,1},{1,2},{2,3},{3,4},{4,5},{5,6},{6,7},{7,8},{8,9},{9,10},{10,1... | collective-permute-start | bytes 2312 | tf_op jit(solution)/shard_map/ppermute | solution.py:15
  167.2 10.6 %collective-permute-start.11 = (s32[192]{0:T(256)S(1)}, s32[192]{0:T(256)S(1)}, u32[]{:S(2)}, u32[]{:S(2)}) collective-permute-start(s32[192]{0:T(256)S(1)} %collective-permute-done.10), channel_id=1, source_target_pairs={{0,1},{1,2},{2,3},{3,4},{4,5},{5,6},{6,7},{7,8},{8,9},{9,10},{10,1... | collective-permute-start | bytes 2312 | tf_op jit(solution)/shard_map/ppermute | solution.py:15
  177.8 10.6 %collective-permute-start.12 = (s32[192]{0:T(256)S(1)}, s32[192]{0:T(256)S(1)}, u32[]{:S(2)}, u32[]{:S(2)}) collective-permute-start(s32[192]{0:T(256)S(1)} %collective-permute-done.11), channel_id=1, source_target_pairs={{0,1},{1,2},{2,3},{3,4},{4,5},{5,6},{6,7},{7,8},{8,9},{9,10},{10,1... | collective-permute-start | bytes 2312 | tf_op jit(solution)/shard_map/ppermute | solution.py:15
  188.4 14.4 %collective-permute-start.13 = (s32[192]{0:T(256)S(1)}, s32[192]{0:T(256)S(1)}, u32[]{:S(2)}, u32[]{:S(2)}) collective-permute-start(s32[192]{0:T(256)S(1)} %collective-permute-done.12), channel_id=1, source_target_pairs={{0,1},{1,2},{2,3},{3,4},{4,5},{5,6},{6,7},{7,8},{8,9},{9,10},{10,1... | collective-permute-start | bytes 2312 | tf_op jit(solution)/shard_map/ppermute | solution.py:15
  367.0 7.3 %copy-start = (bf16[1,192,8192]{2,1,0:T(8,128)(2,1)S(1)}, bf16[1,192,8192]{2,1,0:T(8,128)(2,1)}, u32[]{:S(2)}) copy-start(bf16[1,192,8192]{2,1,0:T(8,128)(2,1)} %param.7) | copy-start | bytes 9437188
  377.8 62.9 %collective-permute-start.14 = (bf16[1,192,8192]{2,1,0:T(8,128)(2,1)S(1)}, bf16[1,192,8192]{2,1,0:T(8,128)(2,1)S(1)}, u32[]{:S(2)}, u32[]{:S(2)}) collective-permute-start(bf16[1,192,8192]{2,1,0:T(8,128)(2,1)S(1)} %add_convert_fusion), channel_id=1, source_target_pairs={{0,128},{128,0},{1,129},{129,1},{2,130},{130,2},{3,131},{131,3},{4... | collective-permute-start | bytes 9437192 | tf_op jit(solution)/shard_map/ppermute | solution.py:20
where the time goes:
time: 445 us; the launch traced here: 442 us
  starting transfers between devices  128 us (29%)
  waiting for transfers between devices  127 us (29%)
  matrix products  113 us (25%)
  local copies, waits for them, and re-layouts  67.5 us (15%)
  other arithmetic  6.51 us (1%)
    ppermute x14, starting transfers between devices, shifted(): return lax.ppermute(value, axis, pairs)  128 us
    ppermute x14, waiting for transfers between devices, shifted(): return lax.ppermute(value, axis, pairs)  64.3 us
    sub x8, matrix products, one_group(): expo = jnp.exp(scores - top_score)  63.6 us
    ppermute x1, waiting for transfers between devices, from_behind(): lax.ppermute(value, axis, [(i, (i + by) % size) for i in range(size)])  62.8 us
    dot_general x8, matrix products, one_group(): jnp.einsum('rtl,ld->trd', probs, value_group, preferred_element_type=jnp....  49.3 us
    ppermute x7, local copies, waits for them, and re-layouts, shifted(): return lax.ppermute(value, axis, pairs)  13.2 us
    concatenate x1, local copies, waits for them, and re-layouts, local(): window_pair = jnp.concatenate(pair_list, axis=0)  11.8 us
    unnamed x16, local copies, waits for them, and re-layouts  11.3 us
  transfers between devices with their start and end apart: 15, of which 13 were waited for; matrix products, arithmetic and copies ran while one was open for 4% of the time, Pallas kernels for 0%

commit v1 on v0

v1 whole, which is shorter than its diff:
```python
import functools

import jax
import jax.numpy as jnp
from jax import lax
from jax.experimental import pallas as pl
from jax.experimental.pallas import tpu as pltpu
from jax.sharding import PartitionSpec as P

MESH = pl.DeviceIdType.MESH
HD = 128
REPEAT = 8
TOK = 192
GROUPS = 4
PIECES = 4
HEADS = REPEAT // PIECES
SEG_ROWS = 16
SLOTS = 9
SCALE = HD ** -0.5 * 1.4426950408889634
MASKED = -1e30


def rows_of(group):
    if group == 0:
        return pl.ds(0, SEG_ROWS + 2 * TOK)
    return pl.ds(SEG_ROWS + 2 * TOK * group, 2 * TOK)


def kernel(ctx, stream_ref, query_ref, key_ref, value_ref, seg_ref, out_ref,
           win, other, qv, sv, ov, bias, loc_sem, kv_send, kv_recv, qs_send, qs_recv, out_send, out_recv):
    s = lax.axis_index("section")
    c = lax.axis_index("ctx")
    k = lax.rem(c, 2)
    h = lax.rem(c // 2, 2)
    cross = 1 - 2 * k
    mate = (s, c + cross)

    def at(offset):
        return (s, lax.rem(c + offset + ctx, ctx))

    x_off = 2 - 4 * h
    barrier = pltpu.get_barrier_semaphore()
    greeted = [mate, at(x_off), at(x_off + cross), (1 - s, c), (1 - s, c + cross)]
    for hop in (4, 8, -4, -8):
        greeted += [at(hop), at(hop + cross)]
    for device in greeted:
        pl.semaphore_signal(barrier, inc=1, device_id=device, device_id_type=MESH)

    def local_kv(g):
        out = []
        for half, (buf, base) in enumerate(((win.at[7 + k], 4 * k), (other, 4 - 4 * k))):
            cols = pl.ds(pl.multiple_of((base + g) * HD, HD), HD)
            for i, ref in enumerate((key_ref, value_ref)):
                rows = pl.ds(SEG_ROWS + 2 * TOK * g + TOK * i, TOK)
                out.append(pltpu.make_async_copy(ref.at[0, :, cols], buf.at[rows], loc_sem.at[2 * half + i, g]))
        return out

    def local_qs(g):
        cols = pl.ds(pl.multiple_of((4 * k + g) * REPEAT * HD, REPEAT * HD), REPEAT * HD)
        return [
            pltpu.make_async_copy(query_ref.at[0, :, cols], qv.at[k, g], loc_sem.at[4, g]),
            pltpu.make_async_copy(stream_ref.at[0, :, cols], sv.at[k, g], loc_sem.at[5, g]),
        ]

    def mate_qs(g):
        cols = pl.ds(pl.multiple_of((4 - 4 * k + g) * REPEAT * HD, REPEAT * HD), REPEAT * HD)
        return [
            pltpu.make_async_remote_copy(
                src_ref=ref.at[0, :, cols], dst_ref=buf.at[k, g], send_sem=qs_send.at[i, g], recv_sem=qs_recv.at[i, g],
                device_id=mate, device_id_type=MESH)
            for i, (ref, buf) in enumerate(((query_ref, qv), (stream_ref, sv)))
        ]

    def kv_copy(src, slot, g, device, sem):
        return pltpu.make_async_remote_copy(
            src_ref=src.at[rows_of(g)], dst_ref=win.at[slot].at[rows_of(g)],
            send_sem=kv_send.at[sem, g], recv_sem=kv_recv.at[slot, g], device_id=device, device_id_type=MESH)

    def arrived(slot, g):
        kv_copy(win.at[slot], slot, g, mate, 0).wait_recv()

    own = win.at[7 + k]

    def sends(g):
        near = [kv_copy(other, 7 + k, g, mate, 0),
                kv_copy(own, 3 + k, g, at(4), 1), kv_copy(other, 3 + k, g, at(4 + cross), 2)]
        far = [kv_copy(own, 0, g, at(8), 3), kv_copy(other, 0, g, at(8 + cross), 4)]
        across = [kv_copy(own, 5 + k, g, at(2), 5), kv_copy(other, 5 + k, g, at(2 + cross), 6)]
        onward = [kv_copy(win.at[3], 5, g, at(-2), 5), kv_copy(win.at[4], 6, g, at(-2), 6)]
        forward = [kv_copy(win.at[5], 1, g, at(4), 7), kv_copy(win.at[6], 2, g, at(4), 8)]
        return near, far, across, onward, forward

    def start(copies):
        for copy in copies:
            copy.start()

    def own_send(g):
        near, far, across, _, _ = sends(g)
        for copy in local_kv(g):
            copy.wait()

        @pl.when(h == 0)
        def _():
            start(across)
        start(near)

        @pl.when(k == 1)
        def _():
            start(far)

    def pass_on(g):
        _, _, _, onward, forward = sends(g)

        @pl.when(h == 1)
        def _():
            for i in range(2):
                arrived(3 + i, g)
                onward[i].start()
        for i in range(2):
            arrived(5 + i, g)
            forward[i].start()

    def rest(g):
        @pl.when(h == 0)
        def _():
            arrived(3, g)
            arrived(4, g)
        arrived(8 - k, g)
        for slot in range(3):
            arrived(slot, g)
        for copy in local_qs(g):
            copy.wait()
        for copy in mate_qs(g):
            copy.wait_recv()

    start(local_kv(0))
    for g in range(GROUPS):
        if g:
            start(local_kv(g))
        start(local_qs(g))

    lane = lax.broadcasted_iota(jnp.int32, (16, 128), 1)
    row = lax.broadcasted_iota(jnp.int32, (16, 128), 0)
    seg = seg_ref[...].astype(jnp.float32)
    first = jnp.broadcast_to(seg[:, :128], (16, 128))
    last = jnp.broadcast_to(jnp.concatenate([seg[:, 128:], jnp.zeros((1, 64), jnp.float32)], axis=1), (16, 128))
    first_moved = pltpu.roll(first, 64, 1)
    last_moved = pltpu.roll(last, 64, 1)
    tile = jnp.where(row == 0, first, jnp.where(row == 1, last, jnp.where(
        row == 2, jnp.where(lane >= 64, first_moved, 0.0), jnp.where(lane < 64, first_moved, last_moved))))
    tile = tile.astype(jnp.bfloat16)
    win[7 + k, pl.ds(0, 16), :] = tile
    other[pl.ds(0, 16), :] = tile

    pl.semaphore_wait(barrier, len(greeted))

    own_send(0)
    for g in range(GROUPS):
        start(mate_qs(g))
    pass_on(0)
    own_send(1)
    rest(0)

    q_row = lax.broadcasted_iota(jnp.int32, (TOK, 128), 0)
    k_lane = lax.broadcasted_iota(jnp.int32, (TOK, 128), 1)
    seg_rows = [win[w, pl.ds(0, 16), :].astype(jnp.float32) for w in range(SLOTS)]
    for j in range(2):
        mine = seg_rows[7 + j]
        column = jnp.sum(
            jnp.where(q_row == k_lane, mine[0:1], 0.0) + jnp.where(q_row == k_lane + 128, mine[1:2], 0.0),
            axis=1, keepdims=True)
        begin = (c - k - 7 + j) * TOK
        for m in range(12):
            a, b = seg_rows[j + 2 * (m // 3)], seg_rows[j + 2 * (m // 3) + 1]
            keys_seg = (a[0:1], a[1:2] + b[2:3], b[3:4])[m % 3]
            seen = (column == keys_seg) & (k_lane + 128 * m <= q_row + 7 * TOK) & (k_lane + 128 * m + begin >= 0)
            bias[j, :, 128 * m:128 * (m + 1)] = jnp.where(seen, 0.0, MASKED)

    def out_copy(j, g, piece, sem):
        cols = pl.ds(pl.multiple_of((4 * k + g) * REPEAT * HD + piece * HEADS * HD, HEADS * HD), HEADS * HD)
        return pltpu.make_async_remote_copy(
            src_ref=ov.at[j, g, piece], dst_ref=out_ref.at[0, :, cols],
            send_sem=out_send.at[sem], recv_sem=out_recv.at[k * GROUPS * PIECES + g * PIECES + piece],
            device_id=(1 - s, c - k + j), device_id_type=MESH)

    def step(t, _):
        g = t // (2 * PIECES)
        j = lax.rem(t // PIECES, 2)
        piece = lax.rem(t, PIECES)
        for i in range(1, GROUPS):
            @pl.when(t == 2 * PIECES * i)
            def _():
                rest(i)

            @pl.when(t == 2 * PIECES * (i - 1) + PIECES)
            def _():
                pass_on(i)
                if i + 1 < GROUPS:
                    own_send(i + 1)

        cols = pl.ds(pl.multiple_of(piece * HEADS * HD, HEADS * HD), HEADS * HD)
        q_two = qv[j, g, :, cols]
        q_rows = jnp.concatenate([q_two[:, i * HD:(i + 1) * HD] for i in range(HEADS)], axis=0)
        at_row = pl.multiple_of(SEG_ROWS + 2 * TOK * g, 16)
        key_rows = win[pl.ds(j, 8), pl.ds(at_row, TOK), :].reshape(8 * TOK, HD)
        value_rows = win[pl.ds(j, 8), pl.ds(pl.multiple_of(at_row + TOK, 16), TOK), :].reshape(8 * TOK, HD)
        score = lax.dot_general(q_rows, key_rows, (((1,), (1,)), ((), ())), preferred_element_type=jnp.float32)
        score = score.reshape(HEADS, TOK, 8 * TOK) + bias[j][None]
        top = jnp.max(score, axis=-1, keepdims=True)
        expo = jnp.exp2((score - top) * SCALE)
        total = jnp.sum(expo, axis=-1, keepdims=True)
        result = jnp.dot(expo.astype(jnp.bfloat16).reshape(HEADS * TOK, 8 * TOK), value_rows,
                         preferred_element_type=jnp.float32)
        result = result.reshape(HEADS, TOK, HD) / total
        before = sv[j, g, :, cols].astype(jnp.float32)
        for i in range(HEADS):
            ov[j, g, piece, :, i * HD:(i + 1) * HD] = (before[:, i * HD:(i + 1) * HD] + result[i]).astype(jnp.bfloat16)
        out_copy(j, g, piece, t).start()
        return 0

    lax.fori_loop(0, 2 * GROUPS * PIECES, step, 0)

    for g in range(GROUPS):
        near, far, across, onward, forward = sends(g)
        for copy in near + across + forward + mate_qs(g):
            copy.wait_send()

        @pl.when(k == 1)
        def _():
            for copy in far:
                copy.wait_send()

    def finish(t, _):
        out_copy(0, 0, 0, t).wait_send()
        pltpu.make_async_remote_copy(
            src_ref=ov.at[0, 0, 0], dst_ref=out_ref.at[0, :, pl.ds(0, HEADS * HD)],
            send_sem=out_send.at[t], recv_sem=out_recv.at[t], device_id=mate, device_id_type=MESH).wait_recv()
        return 0

    lax.fori_loop(0, 2 * GROUPS * PIECES, finish, 0)


def solution(mesh):
    ctx = mesh.shape["ctx"]
    hbm = pl.BlockSpec(memory_space=pl.ANY)

    def local(stream, queries, keys, values, segments):
        copies = 2 * GROUPS * PIECES
        return pl.pallas_call(
            functools.partial(kernel, ctx),
            out_shape=jax.ShapeDtypeStruct(stream.shape, stream.dtype),
            in_specs=[hbm, hbm, hbm, hbm, pl.BlockSpec(memory_space=pltpu.VMEM)],
            out_specs=hbm,
            scratch_shapes=[
                pltpu.VMEM((SLOTS, SEG_ROWS + 2 * TOK * GROUPS, HD), jnp.bfloat16),
                pltpu.VMEM((SEG_ROWS + 2 * TOK * GROUPS, HD), jnp.bfloat16),
                pltpu.VMEM((2, GROUPS, TOK, REPEAT * HD), jnp.bfloat16),
                pltpu.VMEM((2, GROUPS, TOK, REPEAT * HD), jnp.bfloat16),
                pltpu.VMEM((2, GROUPS, PIECES, TOK, HEADS * HD), jnp.bfloat16),
                pltpu.VMEM((2, TOK, 8 * TOK), jnp.float32),
                pltpu.SemaphoreType.DMA((6, GROUPS)),
                pltpu.SemaphoreType.DMA((9, GROUPS)),
                pltpu.SemaphoreType.DMA((SLOTS, GROUPS)),
                pltpu.SemaphoreType.DMA((2, GROUPS)),
                pltpu.SemaphoreType.DMA((2, GROUPS)),
                pltpu.SemaphoreType.DMA((copies,)),
                pltpu.SemaphoreType.DMA((copies,)),
            ],
            compiler_params=pltpu.CompilerParams(
                collective_id=0, has_side_effects=True, vmem_limit_bytes=56 << 20),
        )(stream, queries, keys, values, segments)

    spec = P("section", "ctx", None)
    return jax.shard_map(
        local, mesh=mesh, in_specs=(spec, spec, spec, spec, P("section", "ctx")), out_specs=spec, check_vma=False)
```

time: 445 us -> 122 us (0.27)
  the two profiles are of different devices: /device:TPU:127 before, /device:TPU:1 now
where the time goes in v1:
time: 122 us
  Pallas kernels  118 us (97%)
  local copies, waits for them, and re-layouts  3.86 us (3%)
    pallas_call x1, Pallas kernels, local(): pl.pallas_call(functools.partial(kernel, ctx), out_shape=jax.ShapeDtypeSt...  118 us
    unnamed x1, local copies, waits for them, and re-layouts  3.86 us

profile of v1, /device:TPU:1, one launch (start us, length us, event | category | flops | bytes accessed | tf_op | source)
XLA Modules:
  0.0 121.6 jit_solution(17443664693700071101)
XLA Ops:
  0.0 117.7 %shard_map.55 = bf16[1,192,8192]{2,1,0:T(8,128)(2,1)} custom-call(bf16[1,192,8192]{2,1,0:T(8,128)(2,1)} %stream_ref.1, bf16[1,192,8192]{2,1,0:T(8,128)(2,1)} %query_ref.1, bf16[1,192,1024]{2,1,0:T(8,128)(2,1)} %key_ref.1, bf16[1,192,1024]{2,1,0:T(8,128)(2,1)} %value_ref.1, s32[1,192]{1,0:T(1,128)} %seg_ref.1), custom_call_target="tpu_custom_call" | custom-call | tf_op jit(solution)/shard_map/pallas_call | solution.py:249
  117.7 3.9 %copy.7 = bf16[1,192,8192]{2,1,0:T(8,128)(2,1)} copy(bf16[1,192,8192]{2,1,0:T(8,128)(2,1)} %shard_map.55) | data formatting | bytes 6291456

commit v2 on v1

--- a/solution.py
+++ b/solution.py
@@ -15,7 +15,7 @@
 PIECES = 4
 HEADS = REPEAT // PIECES
 SEG_ROWS = 16
-SLOTS = 9
+SLOTS = 11
 SCALE = HD ** -0.5 * 1.4426950408889634
 MASKED = -1e30
 
@@ -27,24 +27,40 @@
 
 
 def kernel(ctx, stream_ref, query_ref, key_ref, value_ref, seg_ref, out_ref,
-           win, other, qv, sv, ov, bias, loc_sem, kv_send, kv_recv, qs_send, qs_recv, out_send, out_recv):
+           win, other, qv, sv, ov, bias, loc_sem, kv_send, kv_recv, qs_send, qs_recv, out_send, out_recv, ready, seg_own, seg_sem):
     s = lax.axis_index("section")
     c = lax.axis_index("ctx")
     k = lax.rem(c, 2)
     h = lax.rem(c // 2, 2)
+    line = c // 4
+    lines = ctx // 4
     cross = 1 - 2 * k
+    x_off = 2 - 4 * h
+    next1, next2 = line + 1 < lines, line + 2 < lines
+    past1, past2 = line >= 1, line >= 2
+    left = (h == 1) | past1
+    left3 = jnp.where(h == 1, past1, past2)
     mate = (s, c + cross)
 
     def at(offset):
         return (s, lax.rem(c + offset + ctx, ctx))
 
-    x_off = 2 - 4 * h
+    def tell(sem, device):
+        pl.semaphore_signal(sem, inc=1, device_id=device, device_id_type=MESH)
+
     barrier = pltpu.get_barrier_semaphore()
-    greeted = [mate, at(x_off), at(x_off + cross), (1 - s, c), (1 - s, c + cross)]
-    for hop in (4, 8, -4, -8):
-        greeted += [at(hop), at(hop + cross)]
-    for device in greeted:
-        pl.semaphore_signal(barrier, inc=1, device_id=device, device_id_type=MESH)
+    for device in (mate, at(x_off), at(x_off + cross), (1 - s, c), (1 - s, c + cross)):
+        tell(barrier, device)
+
+    @pl.when(next1)
+    def _():
+        tell(barrier, at(4))
+        tell(barrier, at(4 + cross))
+
+    @pl.when(next2 & (k == 1))
+    def _():
+        tell(barrier, at(8))
+        tell(barrier, at(8 + cross))
 
     def local_kv(g):
         out = []
@@ -81,67 +97,92 @@
 
     own = win.at[7 + k]
 
-    def sends(g):
-        near = [kv_copy(other, 7 + k, g, mate, 0),
-                kv_copy(own, 3 + k, g, at(4), 1), kv_copy(other, 3 + k, g, at(4 + cross), 2)]
-        far = [kv_copy(own, 0, g, at(8), 3), kv_copy(other, 0, g, at(8 + cross), 4)]
-        across = [kv_copy(own, 5 + k, g, at(2), 5), kv_copy(other, 5 + k, g, at(2 + cross), 6)]
-        onward = [kv_copy(win.at[3], 5, g, at(-2), 5), kv_copy(win.at[4], 6, g, at(-2), 6)]
-        forward = [kv_copy(win.at[5], 1, g, at(4), 7), kv_copy(win.at[6], 2, g, at(4), 8)]
-        return near, far, across, onward, forward
+    def to_mate(g):
+        return [kv_copy(other, 7 + k, g, mate, 0)]
+
+    def to_next1(g):
+        return [kv_copy(own, 3 + k, g, at(4), 1), kv_copy(other, 3 + k, g, at(4 + cross), 2)]
+
+    def to_next2(g):
+        return [kv_copy(own, 0, g, at(8), 3), kv_copy(other, 0, g, at(8 + cross), 4)]
+
+    def across(g):
+        slot = 5 + 4 * h + k
+        return [kv_copy(own, slot, g, at(x_off), 5), kv_copy(other, slot, g, at(x_off + cross), 6)]
+
+    def onward():
+        return [kv_copy(win.at[3 + i], 5 + i, 0, at(-2), 5 + i) for i in range(2)]
+
+    def lift(g):
+        return [kv_copy(win.at[9 + i], 5 + i, g, at(4), 9 + i) for i in range(2)]
+
+    def forward(g):
+        return [kv_copy(win.at[5 + i], 1 + i, g, at(4), 7 + i) for i in range(2)]
 
     def start(copies):
         for copy in copies:
             copy.start()
 
-    def own_send(g):
-        near, far, across, _, _ = sends(g)
-        for copy in local_kv(g):
-            copy.wait()
-
+    def rows_send(g):
+        @pl.when(next1)
+        def _():
+            start(to_next1(g))
+
+        @pl.when(next2 & (k == 1))
+        def _():
+            start(to_next2(g))
+
+    def pass_up(g):
         @pl.when(h == 0)
         def _():
-            start(across)
-        start(near)
-
-        @pl.when(k == 1)
-        def _():
-            start(far)
+            arrived(9, g)
+            arrived(10, g)
+
+            @pl.when(next1)
+            def _():
+                start(lift(g))
 
     def pass_on(g):
-        _, _, _, onward, forward = sends(g)
-
-        @pl.when(h == 1)
-        def _():
-            for i in range(2):
-                arrived(3 + i, g)
-                onward[i].start()
-        for i in range(2):
-            arrived(5 + i, g)
-            forward[i].start()
-
-    def rest(g):
-        @pl.when(h == 0)
+        @pl.when(left)
+        def _():
+            arrived(5, g)
+            arrived(6, g)
+
+            @pl.when(next1)
+            def _():
+                start(forward(g))
+
+    def rest_near(g):
+        @pl.when(past1 & ((h == 0) | (g > 0)))
         def _():
             arrived(3, g)
             arrived(4, g)
         arrived(8 - k, g)
-        for slot in range(3):
-            arrived(slot, g)
         for copy in local_qs(g):
             copy.wait()
         for copy in mate_qs(g):
             copy.wait_recv()
 
-    start(local_kv(0))
+    def rest_far(g):
+        @pl.when(left3)
+        def _():
+            arrived(1, g)
+            arrived(2, g)
+
+        @pl.when(past2)
+        def _():
+            arrived(0, g)
+
+    seg_copy = pltpu.make_async_copy(seg_ref, seg_own, seg_sem)
+    seg_copy.start()
     for g in range(GROUPS):
-        if g:
-            start(local_kv(g))
+        start(local_kv(g))
         start(local_qs(g))
+    seg_copy.wait()
 
     lane = lax.broadcasted_iota(jnp.int32, (16, 128), 1)
     row = lax.broadcasted_iota(jnp.int32, (16, 128), 0)
-    seg = seg_ref[...].astype(jnp.float32)
+    seg = seg_own[...].astype(jnp.float32)
     first = jnp.broadcast_to(seg[:, :128], (16, 128))
     last = jnp.broadcast_to(jnp.concatenate([seg[:, 128:], jnp.zeros((1, 64), jnp.float32)], axis=1), (16, 128))
     first_moved = pltpu.roll(first, 64, 1)
@@ -152,29 +193,89 @@
     win[7 + k, pl.ds(0, 16), :] = tile
     other[pl.ds(0, 16), :] = tile
 
-    pl.semaphore_wait(barrier, len(greeted))
-
-    own_send(0)
-    for g in range(GROUPS):
+    def clear(slot, _):
+        win[slot] = jnp.zeros(win.shape[1:], win.dtype)
+        return 0
+
+    lax.fori_loop(0, jnp.maximum(7 - 2 * (c // 2), 0), clear, 0)
+
+    pl.semaphore_wait(barrier, 5 + 2 * past1.astype(jnp.int32) + past2.astype(jnp.int32))
+
+    @pl.when(past1)
+    def _():
+        tell(ready.at[0], at(-4))
+        tell(ready.at[0], at(-4 + cross))
+
+    @pl.when(past2)
+    def _():
+        tell(ready.at[1], at(-7 - k))
+
+    for copy in local_kv(0):
+        copy.wait()
+
+    @pl.when(h == 0)
+    def _():
+        start(across(0))
+    start(to_mate(0))
+    start(mate_qs(0))
+
+    @pl.when(next1)
+    def _():
+        pl.semaphore_wait(ready.at[0], 2)
+        start(to_next1(0))
+
+    @pl.when(next2 & (k == 1))
+    def _():
+        pl.semaphore_wait(ready.at[1], 2)
+        start(to_next2(0))
+
+    for g in range(1, GROUPS):
+        for copy in local_kv(g):
+            copy.wait()
+
+    @pl.when(h == 0)
+    def _():
+        for g in range(1, GROUPS):
+            start(across(g))
+
+    @pl.when(h == 1)
+    def _():
+        @pl.when(past1)
+        def _():
+            for i, copy in enumerate(onward()):
+                arrived(3 + i, 0)
+                copy.start()
+        for g in range(1, GROUPS):
+            start(across(g))
+    pass_on(0)
+    for g in range(1, GROUPS):
+        start(to_mate(g))
         start(mate_qs(g))
-    pass_on(0)
-    own_send(1)
-    rest(0)
+    rows_send(1)
+    pass_up(1)
+    rest_near(0)
 
     q_row = lax.broadcasted_iota(jnp.int32, (TOK, 128), 0)
     k_lane = lax.broadcasted_iota(jnp.int32, (TOK, 128), 1)
-    seg_rows = [win[w, pl.ds(0, 16), :].astype(jnp.float32) for w in range(SLOTS)]
+    columns = []
     for j in range(2):
-        mine = seg_rows[7 + j]
-        column = jnp.sum(
+        mine = win[7 + j, pl.ds(0, 16), :].astype(jnp.float32)
+        columns.append(jnp.sum(
             jnp.where(q_row == k_lane, mine[0:1], 0.0) + jnp.where(q_row == k_lane + 128, mine[1:2], 0.0),
-            axis=1, keepdims=True)
-        begin = (c - k - 7 + j) * TOK
-        for m in range(12):
-            a, b = seg_rows[j + 2 * (m // 3)], seg_rows[j + 2 * (m // 3) + 1]
-            keys_seg = (a[0:1], a[1:2] + b[2:3], b[3:4])[m % 3]
-            seen = (column == keys_seg) & (k_lane + 128 * m <= q_row + 7 * TOK) & (k_lane + 128 * m + begin >= 0)
-            bias[j, :, 128 * m:128 * (m + 1)] = jnp.where(seen, 0.0, MASKED)
+            axis=1, keepdims=True))
+
+    def mask(pairs):
+        for j, pair in pairs:
+            a, b = (win[j + 2 * pair + i, pl.ds(0, 16), :].astype(jnp.float32) for i in range(2))
+            begin = (c - k - 7 + j) * TOK
+            for i, keys_seg in enumerate((a[0:1], a[1:2] + b[2:3], b[3:4])):
+                m = 3 * pair + i
+                seen = (columns[j] == keys_seg) & (k_lane + 128 * m <= q_row + 7 * TOK) & (k_lane + 128 * m + begin >= 0)
+                bias[j, :, 128 * m:128 * (m + 1)] = jnp.where(seen, 0.0, MASKED)
+
+    mask(((0, 2), (0, 3), (1, 1), (1, 2), (1, 3)))
+    rest_far(0)
+    mask(((0, 0), (0, 1), (1, 0)))
 
     def out_copy(j, g, piece, sem):
         cols = pl.ds(pl.multiple_of((4 * k + g) * REPEAT * HD + piece * HEADS * HD, HEADS * HD), HEADS * HD)
@@ -190,13 +291,15 @@
         for i in range(1, GROUPS):
             @pl.when(t == 2 * PIECES * i)
             def _():
-                rest(i)
+                rest_near(i)
+                rest_far(i)
 
             @pl.when(t == 2 * PIECES * (i - 1) + PIECES)
             def _():
                 pass_on(i)
                 if i + 1 < GROUPS:
-                    own_send(i + 1)
+                    rows_send(i + 1)
+                    pass_up(i + 1)
 
         cols = pl.ds(pl.multiple_of(piece * HEADS * HD, HEADS * HD), HEADS * HD)
         q_two = qv[j, g, :, cols]
@@ -220,15 +323,32 @@
 
     lax.fori_loop(0, 2 * GROUPS * PIECES, step, 0)
 
+    def sent(copies):
+        for copy in copies:
+            copy.wait_send()
+
     for g in range(GROUPS):
-        near, far, across, onward, forward = sends(g)
-        for copy in near + across + forward + mate_qs(g):
-            copy.wait_send()
-
-        @pl.when(k == 1)
-        def _():
-            for copy in far:
-                copy.wait_send()
+        sent(to_mate(g) + mate_qs(g))
+
+        @pl.when((h == 0) | ((g > 0) | past1))
+        def _():
+            sent(across(g))
+
+        @pl.when(next1)
+        def _():
+            sent(to_next1(g))
+            if g:
+                @pl.when(h == 0)
+                def _():
+                    sent(lift(g))
+
+            @pl.when(left)
+            def _():
+                sent(forward(g))
+
+        @pl.when(next2 & (k == 1))
+        def _():
+            sent(to_next2(g))
 
     def finish(t, _):
         out_copy(0, 0, 0, t).wait_send()
@@ -242,15 +362,15 @@
 
 def solution(mesh):
     ctx = mesh.shape["ctx"]
-    hbm = pl.BlockSpec(memory_space=pl.ANY)
+    hbm = pl.BlockSpec(memory_space=pltpu.HBM)
 
     def local(stream, queries, keys, values, segments):
         copies = 2 * GROUPS * PIECES
         return pl.pallas_call(
             functools.partial(kernel, ctx),
             out_shape=jax.ShapeDtypeStruct(stream.shape, stream.dtype),
-            in_specs=[hbm, hbm, hbm, hbm, pl.BlockSpec(memory_space=pltpu.VMEM)],
-            out_specs=hbm,
+            in_specs=[hbm] * 5,
+            out_specs=pl.BlockSpec(memory_space=pltpu.VMEM),
             scratch_shapes=[
                 pltpu.VMEM((SLOTS, SEG_ROWS + 2 * TOK * GROUPS, HD), jnp.bfloat16),
                 pltpu.VMEM((SEG_ROWS + 2 * TOK * GROUPS, HD), jnp.bfloat16),
@@ -259,16 +379,19 @@
                 pltpu.VMEM((2, GROUPS, PIECES, TOK, HEADS * HD), jnp.bfloat16),
                 pltpu.VMEM((2, TOK, 8 * TOK), jnp.float32),
                 pltpu.SemaphoreType.DMA((6, GROUPS)),
-                pltpu.SemaphoreType.DMA((9, GROUPS)),
+                pltpu.SemaphoreType.DMA((11, GROUPS)),
                 pltpu.SemaphoreType.DMA((SLOTS, GROUPS)),
                 pltpu.SemaphoreType.DMA((2, GROUPS)),
                 pltpu.SemaphoreType.DMA((2, GROUPS)),
                 pltpu.SemaphoreType.DMA((copies,)),
                 pltpu.SemaphoreType.DMA((copies,)),
+                pltpu.SemaphoreType.REGULAR((2,)),
+                pltpu.VMEM((1, TOK), jnp.int32),
+                pltpu.SemaphoreType.DMA,
             ],
             compiler_params=pltpu.CompilerParams(
-                collective_id=0, has_side_effects=True, vmem_limit_bytes=56 << 20),
-        )(stream, queries, keys, values, segments)
+                collective_id=0, has_side_effects=True, vmem_limit_bytes=40 << 20),
+        )(*[pltpu.with_memory_space_constraint(a, pltpu.HBM) for a in (stream, queries, keys, values, segments)])
 
     spec = P("section", "ctx", None)
     return jax.shard_map(

time: 122 us -> 105 us (0.86)
  the two profiles are of different devices: /device:TPU:1 before, /device:TPU:193 now
where the time goes in v2:
time: 105 us
  Pallas kernels  104 us (99%)
  local copies, waits for them, and re-layouts  1.67 us (2%)
    pallas_call x1, Pallas kernels, local(): pl.pallas_call(functools.partial(kernel, ctx), out_shape=jax.ShapeDtypeSt...  104 us

profile of v2, /device:TPU:193, one launch (start us, length us, event | category | flops | bytes accessed | tf_op | source)
XLA Modules:
  0.0 105.4 jit_solution(18146497284059803721)
XLA Ops:
  0.0 103.7 %shard_map.55 = bf16[1,192,8192]{2,1,0:T(8,128)(2,1)S(1)} custom-call(bf16[1,192,8192]{2,1,0:T(8,128)(2,1)} %stream_ref.1, bf16[1,192,8192]{2,1,0:T(8,128)(2,1)} %query_ref.1, bf16[1,192,1024]{2,1,0:T(8,128)(2,1)} %key_ref.1, bf16[1,192,1024]{2,1,0:T(8,128)(2,1)} %value_ref.1, s32[1,192]{1,0:T(1,128)} %seg_ref.1), custom_call_target="tpu_custom_call" | custom-call | tf_op jit(solution)/shard_map/pallas_call | solution.py:369
  103.7 1.7 %copy.7 = bf16[1,192,8192]{2,1,0:T(8,128)(2,1)} copy(bf16[1,192,8192]{2,1,0:T(8,128)(2,1)S(1)} %shard_map.55) | data formatting | bytes 6291456

commit v3 on v2

--- a/solution.py
+++ b/solution.py
@@ -12,7 +12,7 @@
 REPEAT = 8
 TOK = 192
 GROUPS = 4
-PIECES = 4
+PIECES = 2
 HEADS = REPEAT // PIECES
 SEG_ROWS = 16
 SLOTS = 11
@@ -27,7 +27,7 @@
 
 
 def kernel(ctx, stream_ref, query_ref, key_ref, value_ref, seg_ref, out_ref,
-           win, other, qv, sv, ov, bias, loc_sem, kv_send, kv_recv, qs_send, qs_recv, out_send, out_recv, ready, seg_own, seg_sem):
+           win, other, qv, sv, ov, bias, loc_sem, kv_send, kv_recv, qs_send, qs_recv, out_send, out_recv, seg_own, seg_sem):
     s = lax.axis_index("section")
     c = lax.axis_index("ctx")
     k = lax.rem(c, 2)
@@ -52,15 +52,15 @@
     for device in (mate, at(x_off), at(x_off + cross), (1 - s, c), (1 - s, c + cross)):
         tell(barrier, device)
 
-    @pl.when(next1)
-    def _():
-        tell(barrier, at(4))
-        tell(barrier, at(4 + cross))
-
-    @pl.when(next2 & (k == 1))
-    def _():
-        tell(barrier, at(8))
-        tell(barrier, at(8 + cross))
+    for there, offsets in (
+        (next1, (4, 4 + cross)), (past1, (-4, -4 + cross)),
+        (next2 & (k == 1), (8, 8 + cross)), (past2, (-7 - k,)),
+        (next1 & (h == 1), (2, 2 + cross)), (past1 & (h == 0), (-2, -2 + cross)),
+    ):
+        @pl.when(there)
+        def _():
+            for offset in offsets:
+                tell(barrier, at(offset))
 
     def local_kv(g):
         out = []
@@ -110,8 +110,8 @@
         slot = 5 + 4 * h + k
         return [kv_copy(own, slot, g, at(x_off), 5), kv_copy(other, slot, g, at(x_off + cross), 6)]
 
-    def onward():
-        return [kv_copy(win.at[3 + i], 5 + i, 0, at(-2), 5 + i) for i in range(2)]
+    def to_next_first():
+        return [kv_copy(own, 5 + k, 0, at(2), 5), kv_copy(other, 5 + k, 0, at(2 + cross), 6)]
 
     def lift(g):
         return [kv_copy(win.at[9 + i], 5 + i, g, at(4), 9 + i) for i in range(2)]
@@ -153,7 +153,7 @@
                 start(forward(g))
 
     def rest_near(g):
-        @pl.when(past1 & ((h == 0) | (g > 0)))
+        @pl.when(past1)
         def _():
             arrived(3, g)
             arrived(4, g)
@@ -199,16 +199,11 @@
 
     lax.fori_loop(0, jnp.maximum(7 - 2 * (c // 2), 0), clear, 0)
 
-    pl.semaphore_wait(barrier, 5 + 2 * past1.astype(jnp.int32) + past2.astype(jnp.int32))
-
-    @pl.when(past1)
-    def _():
-        tell(ready.at[0], at(-4))
-        tell(ready.at[0], at(-4 + cross))
-
-    @pl.when(past2)
-    def _():
-        tell(ready.at[1], at(-7 - k))
+    def count(flag, times):
+        return times * flag.astype(jnp.int32)
+
+    pl.semaphore_wait(barrier, 5 + count(next1, 2) + count(past1, 2) + count(next2 & (k == 1), 2) + count(past2, 1)
+                      + count(next1 & (h == 1), 2) + count(past1 & (h == 0), 2))
 
     for copy in local_kv(0):
         copy.wait()
@@ -216,43 +211,31 @@
     @pl.when(h == 0)
     def _():
         start(across(0))
+
+    @pl.when(next1 & (h == 1))
+    def _():
+        start(to_next_first())
     start(to_mate(0))
     start(mate_qs(0))
 
     @pl.when(next1)
     def _():
-        pl.semaphore_wait(ready.at[0], 2)
         start(to_next1(0))
 
     @pl.when(next2 & (k == 1))
     def _():
-        pl.semaphore_wait(ready.at[1], 2)
         start(to_next2(0))
 
     for g in range(1, GROUPS):
         for copy in local_kv(g):
             copy.wait()
-
-    @pl.when(h == 0)
-    def _():
-        for g in range(1, GROUPS):
-            start(across(g))
-
-    @pl.when(h == 1)
-    def _():
-        @pl.when(past1)
-        def _():
-            for i, copy in enumerate(onward()):
-                arrived(3 + i, 0)
-                copy.start()
-        for g in range(1, GROUPS):
-            start(across(g))
+        start(across(g))
     pass_on(0)
+    pass_up(1)
+    rows_send(1)
     for g in range(1, GROUPS):
         start(to_mate(g))
         start(mate_qs(g))
-    rows_send(1)
-    pass_up(1)
     rest_near(0)
 
     q_row = lax.broadcasted_iota(jnp.int32, (TOK, 128), 0)
@@ -294,30 +277,34 @@
                 rest_near(i)
                 rest_far(i)
 
-            @pl.when(t == 2 * PIECES * (i - 1) + PIECES)
+            @pl.when(t == 2 * PIECES * (i - 1) + 1)
             def _():
                 pass_on(i)
                 if i + 1 < GROUPS:
+                    pass_up(i + 1)
                     rows_send(i + 1)
-                    pass_up(i + 1)
 
         cols = pl.ds(pl.multiple_of(piece * HEADS * HD, HEADS * HD), HEADS * HD)
-        q_two = qv[j, g, :, cols]
-        q_rows = jnp.concatenate([q_two[:, i * HD:(i + 1) * HD] for i in range(HEADS)], axis=0)
         at_row = pl.multiple_of(SEG_ROWS + 2 * TOK * g, 16)
         key_rows = win[pl.ds(j, 8), pl.ds(at_row, TOK), :].reshape(8 * TOK, HD)
         value_rows = win[pl.ds(j, 8), pl.ds(pl.multiple_of(at_row + TOK, 16), TOK), :].reshape(8 * TOK, HD)
-        score = lax.dot_general(q_rows, key_rows, (((1,), (1,)), ((), ())), preferred_element_type=jnp.float32)
-        score = score.reshape(HEADS, TOK, 8 * TOK) + bias[j][None]
-        top = jnp.max(score, axis=-1, keepdims=True)
-        expo = jnp.exp2((score - top) * SCALE)
-        total = jnp.sum(expo, axis=-1, keepdims=True)
-        result = jnp.dot(expo.astype(jnp.bfloat16).reshape(HEADS * TOK, 8 * TOK), value_rows,
-                         preferred_element_type=jnp.float32)
-        result = result.reshape(HEADS, TOK, HD) / total
+        q_all = qv[j, g, :, cols]
         before = sv[j, g, :, cols].astype(jnp.float32)
+
+        def score_of(i):
+            score = lax.dot_general(
+                q_all[:, i * HD:(i + 1) * HD], key_rows, (((1,), (1,)), ((), ())), preferred_element_type=jnp.float32)
+            return score + bias[j]
+
+        score = score_of(0)
         for i in range(HEADS):
-            ov[j, g, piece, :, i * HD:(i + 1) * HD] = (before[:, i * HD:(i + 1) * HD] + result[i]).astype(jnp.bfloat16)
+            later = score_of(i + 1) if i + 1 < HEADS else None
+            top = jnp.max(score, axis=-1, keepdims=True)
+            expo = jnp.exp2((score - top) * SCALE)
+            total = jnp.sum(expo, axis=-1, keepdims=True)
+            result = jnp.dot(expo.astype(jnp.bfloat16), value_rows, preferred_element_type=jnp.float32) / total
+            ov[j, g, piece, :, i * HD:(i + 1) * HD] = (before[:, i * HD:(i + 1) * HD] + result).astype(jnp.bfloat16)
+            score = later
         out_copy(j, g, piece, t).start()
         return 0
 
@@ -330,9 +317,12 @@
     for g in range(GROUPS):
         sent(to_mate(g) + mate_qs(g))
 
-        @pl.when((h == 0) | ((g > 0) | past1))
-        def _():
+        if g:
             sent(across(g))
+        else:
+            @pl.when((h == 0) | next1)
+            def _():
+                sent(across(0))
 
         @pl.when(next1)
         def _():
@@ -385,7 +375,6 @@
                 pltpu.SemaphoreType.DMA((2, GROUPS)),
                 pltpu.SemaphoreType.DMA((copies,)),
                 pltpu.SemaphoreType.DMA((copies,)),
-                pltpu.SemaphoreType.REGULAR((2,)),
                 pltpu.VMEM((1, TOK), jnp.int32),
                 pltpu.SemaphoreType.DMA,
             ],

time: 105 us -> 102 us (0.971)
  the two profiles are of different devices: /device:TPU:193 before, /device:TPU:197 now
where the time goes in v3:
time: 102 us
  Pallas kernels  100 us (98%)
  local copies, waits for them, and re-layouts  1.67 us (2%)
    pallas_call x1, Pallas kernels, local(): pl.pallas_call(functools.partial(kernel, ctx), out_shape=jax.ShapeDtypeSt...  100 us

profile of v3, /device:TPU:197, one launch (start us, length us, event | category | flops | bytes accessed | tf_op | source)
XLA Modules:
  0.0 102.1 jit_solution(18438175725775277480)
XLA Ops:
  0.0 100.4 %shard_map.55 = bf16[1,192,8192]{2,1,0:T(8,128)(2,1)S(1)} custom-call(bf16[1,192,8192]{2,1,0:T(8,128)(2,1)} %stream_ref.1, bf16[1,192,8192]{2,1,0:T(8,128)(2,1)} %query_ref.1, bf16[1,192,1024]{2,1,0:T(8,128)(2,1)} %key_ref.1, bf16[1,192,1024]{2,1,0:T(8,128)(2,1)} %value_ref.1, s32[1,192]{1,0:T(1,128)} %seg_ref.1), custom_call_target="tpu_custom_call" | custom-call | tf_op jit(solution)/shard_map/pallas_call | solution.py:359
  100.4 1.7 %copy.7 = bf16[1,192,8192]{2,1,0:T(8,128)(2,1)} copy(bf16[1,192,8192]{2,1,0:T(8,128)(2,1)S(1)} %shard_map.55) | data formatting | bytes 6291456

commit v4 on v3

--- a/solution.py
+++ b/solution.py
@@ -14,16 +14,21 @@
 GROUPS = 4
 PIECES = 2
 HEADS = REPEAT // PIECES
+PARTS = REPEAT // 2
+WIDE = 2 * HD
 SEG_ROWS = 16
+CHUNKS = ((0, 4), (1,), (2,), (3,))
 SLOTS = 11
 SCALE = HD ** -0.5 * 1.4426950408889634
 MASKED = -1e30
 
 
-def rows_of(group):
-    if group == 0:
-        return pl.ds(0, SEG_ROWS + 2 * TOK)
-    return pl.ds(SEG_ROWS + 2 * TOK * group, 2 * TOK)
+def rows_of(chunk):
+    if chunk == 0:
+        return pl.ds(0, SEG_ROWS + TOK)
+    if chunk == GROUPS:
+        return pl.ds(SEG_ROWS + TOK, TOK)
+    return pl.ds(SEG_ROWS + 2 * TOK * chunk, 2 * TOK)
 
 
 def kernel(ctx, stream_ref, query_ref, key_ref, value_ref, seg_ref, out_ref,
@@ -36,7 +41,7 @@
     lines = ctx // 4
     cross = 1 - 2 * k
     x_off = 2 - 4 * h
-    next1, next2 = line + 1 < lines, line + 2 < lines
+    next1 = line + 1 < lines
     past1, past2 = line >= 1, line >= 2
     left = (h == 1) | past1
     left3 = jnp.where(h == 1, past1, past2)
@@ -54,7 +59,6 @@
 
     for there, offsets in (
         (next1, (4, 4 + cross)), (past1, (-4, -4 + cross)),
-        (next2 & (k == 1), (8, 8 + cross)), (past2, (-7 - k,)),
         (next1 & (h == 1), (2, 2 + cross)), (past1 & (h == 0), (-2, -2 + cross)),
     ):
         @pl.when(there)
@@ -103,15 +107,15 @@
     def to_next1(g):
         return [kv_copy(own, 3 + k, g, at(4), 1), kv_copy(other, 3 + k, g, at(4 + cross), 2)]
 
-    def to_next2(g):
-        return [kv_copy(own, 0, g, at(8), 3), kv_copy(other, 0, g, at(8 + cross), 4)]
+    def far(n):
+        return [kv_copy(win.at[4], 0, n, at(4), 3)]
 
     def across(g):
         slot = 5 + 4 * h + k
         return [kv_copy(own, slot, g, at(x_off), 5), kv_copy(other, slot, g, at(x_off + cross), 6)]
 
-    def to_next_first():
-        return [kv_copy(own, 5 + k, 0, at(2), 5), kv_copy(other, 5 + k, 0, at(2 + cross), 6)]
+    def to_next_first(n):
+        return [kv_copy(own, 5 + k, n, at(2), 5), kv_copy(other, 5 + k, n, at(2 + cross), 6)]
 
     def lift(g):
         return [kv_copy(win.at[9 + i], 5 + i, g, at(4), 9 + i) for i in range(2)]
@@ -126,11 +130,8 @@
     def rows_send(g):
         @pl.when(next1)
         def _():
-            start(to_next1(g))
-
-        @pl.when(next2 & (k == 1))
-        def _():
-            start(to_next2(g))
+            for n in CHUNKS[g]:
+                start(to_next1(n))
 
     def pass_up(g):
         @pl.when(h == 0)
@@ -143,35 +144,45 @@
                 start(lift(g))
 
     def pass_on(g):
+        @pl.when(past1)
+        def _():
+            for n in CHUNKS[g]:
+                arrived(4, n)
+
+                @pl.when(next1)
+                def _():
+                    start(far(n))
+
         @pl.when(left)
         def _():
-            arrived(5, g)
-            arrived(6, g)
-
-            @pl.when(next1)
-            def _():
-                start(forward(g))
+            for n in CHUNKS[g]:
+                for i in range(2):
+                    arrived(5 + i, n)
+
+                    @pl.when(next1)
+                    def _():
+                        start(forward(n)[i:i + 1])
 
     def rest_near(g):
-        @pl.when(past1)
-        def _():
-            arrived(3, g)
-            arrived(4, g)
-        arrived(8 - k, g)
+        for n in CHUNKS[g]:
+            @pl.when(past1)
+            def _():
+                arrived(3, n)
+            arrived(8 - k, n)
         for copy in local_qs(g):
             copy.wait()
         for copy in mate_qs(g):
             copy.wait_recv()
 
-    def rest_far(g):
+    def rest_far(n):
         @pl.when(left3)
         def _():
-            arrived(1, g)
-            arrived(2, g)
+            arrived(1, n)
+            arrived(2, n)
 
         @pl.when(past2)
         def _():
-            arrived(0, g)
+            arrived(0, n)
 
     seg_copy = pltpu.make_async_copy(seg_ref, seg_own, seg_sem)
     seg_copy.start()
@@ -202,29 +213,24 @@
     def count(flag, times):
         return times * flag.astype(jnp.int32)
 
-    pl.semaphore_wait(barrier, 5 + count(next1, 2) + count(past1, 2) + count(next2 & (k == 1), 2) + count(past2, 1)
+    pl.semaphore_wait(barrier, 5 + count(next1, 2) + count(past1, 2)
                       + count(next1 & (h == 1), 2) + count(past1 & (h == 0), 2))
 
     for copy in local_kv(0):
         copy.wait()
 
-    @pl.when(h == 0)
-    def _():
-        start(across(0))
-
-    @pl.when(next1 & (h == 1))
-    def _():
-        start(to_next_first())
-    start(to_mate(0))
+    for n in CHUNKS[0]:
+        @pl.when(h == 0)
+        def _():
+            start(across(n))
+
+        @pl.when(next1 & (h == 1))
+        def _():
+            start(to_next_first(n))
+    for n in CHUNKS[0]:
+        start(to_mate(n))
     start(mate_qs(0))
-
-    @pl.when(next1)
-    def _():
-        start(to_next1(0))
-
-    @pl.when(next2 & (k == 1))
-    def _():
-        start(to_next2(0))
+    rows_send(0)
 
     for g in range(1, GROUPS):
         for copy in local_kv(g):
@@ -259,12 +265,13 @@
     mask(((0, 2), (0, 3), (1, 1), (1, 2), (1, 3)))
     rest_far(0)
     mask(((0, 0), (0, 1), (1, 0)))
-
-    def out_copy(j, g, piece, sem):
-        cols = pl.ds(pl.multiple_of((4 * k + g) * REPEAT * HD + piece * HEADS * HD, HEADS * HD), HEADS * HD)
+    rest_far(GROUPS)
+
+    def out_copy(j, g, part, sem):
+        cols = pl.ds(pl.multiple_of((4 * k + g) * REPEAT * HD + part * WIDE, WIDE), WIDE)
         return pltpu.make_async_remote_copy(
-            src_ref=ov.at[j, g, piece], dst_ref=out_ref.at[0, :, cols],
-            send_sem=out_send.at[sem], recv_sem=out_recv.at[k * GROUPS * PIECES + g * PIECES + piece],
+            src_ref=ov.at[j, g, part], dst_ref=out_ref.at[0, :, cols],
+            send_sem=out_send.at[sem], recv_sem=out_recv.at[(k * GROUPS + g) * PARTS + part],
             device_id=(1 - s, c - k + j), device_id_type=MESH)
 
     def step(t, _):
@@ -303,9 +310,12 @@
             expo = jnp.exp2((score - top) * SCALE)
             total = jnp.sum(expo, axis=-1, keepdims=True)
             result = jnp.dot(expo.astype(jnp.bfloat16), value_rows, preferred_element_type=jnp.float32) / total
-            ov[j, g, piece, :, i * HD:(i + 1) * HD] = (before[:, i * HD:(i + 1) * HD] + result).astype(jnp.bfloat16)
+            part = 2 * piece + i // 2
+            half = (i % 2) * HD
+            ov[j, g, part, :, half:half + HD] = (before[:, i * HD:(i + 1) * HD] + result).astype(jnp.bfloat16)
+            if i % 2:
+                out_copy(j, g, part, 2 * t + i // 2).start()
             score = later
-        out_copy(j, g, piece, t).start()
         return 0
 
     lax.fori_loop(0, 2 * GROUPS * PIECES, step, 0)
@@ -315,39 +325,40 @@
             copy.wait_send()
 
     for g in range(GROUPS):
-        sent(to_mate(g) + mate_qs(g))
-
-        if g:
-            sent(across(g))
-        else:
-            @pl.when((h == 0) | next1)
-            def _():
-                sent(across(0))
-
-        @pl.when(next1)
-        def _():
-            sent(to_next1(g))
+        sent(mate_qs(g))
+        for n in CHUNKS[g]:
+            sent(to_mate(n))
             if g:
-                @pl.when(h == 0)
+                sent(across(n))
+            else:
+                @pl.when((h == 0) | next1)
                 def _():
-                    sent(lift(g))
-
-            @pl.when(left)
-            def _():
-                sent(forward(g))
-
-        @pl.when(next2 & (k == 1))
-        def _():
-            sent(to_next2(g))
+                    sent(across(n))
+
+            @pl.when(next1)
+            def _():
+                sent(to_next1(n))
+                if g:
+                    @pl.when(h == 0)
+                    def _():
+                        sent(lift(n))
+
+                @pl.when(left)
+                def _():
+                    sent(forward(n))
+
+            @pl.when(next1 & past1)
+            def _():
+                sent(far(n))
 
     def finish(t, _):
         out_copy(0, 0, 0, t).wait_send()
         pltpu.make_async_remote_copy(
-            src_ref=ov.at[0, 0, 0], dst_ref=out_ref.at[0, :, pl.ds(0, HEADS * HD)],
+            src_ref=ov.at[0, 0, 0], dst_ref=out_ref.at[0, :, pl.ds(0, WIDE)],
             send_sem=out_send.at[t], recv_sem=out_recv.at[t], device_id=mate, device_id_type=MESH).wait_recv()
         return 0
 
-    lax.fori_loop(0, 2 * GROUPS * PIECES, finish, 0)
+    lax.fori_loop(0, 2 * GROUPS * PARTS, finish, 0)
 
 
 def solution(mesh):
@@ -355,7 +366,7 @@
     hbm = pl.BlockSpec(memory_space=pltpu.HBM)
 
     def local(stream, queries, keys, values, segments):
-        copies = 2 * GROUPS * PIECES
+        copies = 2 * GROUPS * PARTS
         return pl.pallas_call(
             functools.partial(kernel, ctx),
             out_shape=jax.ShapeDtypeStruct(stream.shape, stream.dtype),
@@ -366,11 +377,11 @@
                 pltpu.VMEM((SEG_ROWS + 2 * TOK * GROUPS, HD), jnp.bfloat16),
                 pltpu.VMEM((2, GROUPS, TOK, REPEAT * HD), jnp.bfloat16),
                 pltpu.VMEM((2, GROUPS, TOK, REPEAT * HD), jnp.bfloat16),
-                pltpu.VMEM((2, GROUPS, PIECES, TOK, HEADS * HD), jnp.bfloat16),
+                pltpu.VMEM((2, GROUPS, PARTS, TOK, WIDE), jnp.bfloat16),
                 pltpu.VMEM((2, TOK, 8 * TOK), jnp.float32),
                 pltpu.SemaphoreType.DMA((6, GROUPS)),
-                pltpu.SemaphoreType.DMA((11, GROUPS)),
-                pltpu.SemaphoreType.DMA((SLOTS, GROUPS)),
+                pltpu.SemaphoreType.DMA((11, GROUPS + 1)),
+                pltpu.SemaphoreType.DMA((SLOTS, GROUPS + 1)),
                 pltpu.SemaphoreType.DMA((2, GROUPS)),
                 pltpu.SemaphoreType.DMA((2, GROUPS)),
                 pltpu.SemaphoreType.DMA((copies,)),

time: 102 us -> 98.8 us (0.969)
  the two profiles are of different devices: /device:TPU:197 before, /device:TPU:193 now
where the time goes in v4:
time: 98.8 us; the launch traced here: 98.4 us
  Pallas kernels  96.7 us (98%)
  local copies, waits for them, and re-layouts  1.67 us (2%)
    pallas_call x1, Pallas kernels, local(): pl.pallas_call(functools.partial(kernel, ctx), out_shape=jax.ShapeDtypeSt...  96.7 us

profile of v4, /device:TPU:193, one launch (start us, length us, event | category | flops | bytes accessed | tf_op | source)
XLA Modules:
  0.0 98.4 jit_solution(16342539057472594221)
XLA Ops:
  0.0 96.7 %shard_map.55 = bf16[1,192,8192]{2,1,0:T(8,128)(2,1)S(1)} custom-call(bf16[1,192,8192]{2,1,0:T(8,128)(2,1)} %stream_ref.1, bf16[1,192,8192]{2,1,0:T(8,128)(2,1)} %query_ref.1, bf16[1,192,1024]{2,1,0:T(8,128)(2,1)} %key_ref.1, bf16[1,192,1024]{2,1,0:T(8,128)(2,1)} %value_ref.1, s32[1,192]{1,0:T(1,128)} %seg_ref.1), custom_call_target="tpu_custom_call" | custom-call | tf_op jit(solution)/shard_map/pallas_call | solution.py:370
  96.7 1.7 %copy.7 = bf16[1,192,8192]{2,1,0:T(8,128)(2,1)} copy(bf16[1,192,8192]{2,1,0:T(8,128)(2,1)S(1)} %shard_map.55) | data formatting | bytes 6291456

commit v5 on v4

--- a/solution.py
+++ b/solution.py
@@ -17,15 +17,17 @@
 PARTS = REPEAT // 2
 WIDE = 2 * HD
 SEG_ROWS = 16
-CHUNKS = ((0, 4), (1,), (2,), (3,))
+CHUNKS = ((5, 0, 4), (1,), (2,), (3,))
 SLOTS = 11
 SCALE = HD ** -0.5 * 1.4426950408889634
 MASKED = -1e30
 
 
 def rows_of(chunk):
+    if chunk == GROUPS + 1:
+        return pl.ds(0, SEG_ROWS)
     if chunk == 0:
-        return pl.ds(0, SEG_ROWS + TOK)
+        return pl.ds(SEG_ROWS, TOK)
     if chunk == GROUPS:
         return pl.ds(SEG_ROWS + TOK, TOK)
     return pl.ds(SEG_ROWS + 2 * TOK * chunk, 2 * TOK)
@@ -263,8 +265,9 @@
                 bias[j, :, 128 * m:128 * (m + 1)] = jnp.where(seen, 0.0, MASKED)
 
     mask(((0, 2), (0, 3), (1, 1), (1, 2), (1, 3)))
+    rest_far(GROUPS + 1)
+    mask(((0, 0), (0, 1), (1, 0)))
     rest_far(0)
-    mask(((0, 0), (0, 1), (1, 0)))
     rest_far(GROUPS)
 
     def out_copy(j, g, part, sem):
@@ -380,8 +383,8 @@
                 pltpu.VMEM((2, GROUPS, PARTS, TOK, WIDE), jnp.bfloat16),
                 pltpu.VMEM((2, TOK, 8 * TOK), jnp.float32),
                 pltpu.SemaphoreType.DMA((6, GROUPS)),
-                pltpu.SemaphoreType.DMA((11, GROUPS + 1)),
-                pltpu.SemaphoreType.DMA((SLOTS, GROUPS + 1)),
+                pltpu.SemaphoreType.DMA((11, GROUPS + 2)),
+                pltpu.SemaphoreType.DMA((SLOTS, GROUPS + 2)),
                 pltpu.SemaphoreType.DMA((2, GROUPS)),
                 pltpu.SemaphoreType.DMA((2, GROUPS)),
                 pltpu.SemaphoreType.DMA((copies,)),

time: 98.8 us -> 99 us (level)
  no operation moved by 1% of the time
where the time goes in v5:
time: 99 us; the launch traced here: 98.6 us
  Pallas kernels  96.9 us (98%)
  local copies, waits for them, and re-layouts  1.67 us (2%)
    pallas_call x1, Pallas kernels, local(): pl.pallas_call(functools.partial(kernel, ctx), out_shape=jax.ShapeDtypeSt...  96.9 us

profile of v5, /device:TPU:193, one launch (start us, length us, event | category | flops | bytes accessed | tf_op | source)
XLA Modules:
  0.0 98.6 jit_solution(16692383900803652033)
XLA Ops:
  0.0 96.9 %shard_map.55 = bf16[1,192,8192]{2,1,0:T(8,128)(2,1)S(1)} custom-call(bf16[1,192,8192]{2,1,0:T(8,128)(2,1)} %stream_ref.1, bf16[1,192,8192]{2,1,0:T(8,128)(2,1)} %query_ref.1, bf16[1,192,1024]{2,1,0:T(8,128)(2,1)} %key_ref.1, bf16[1,192,1024]{2,1,0:T(8,128)(2,1)} %value_ref.1, s32[1,192]{1,0:T(1,128)} %seg_ref.1), custom_call_target="tpu_custom_call" | custom-call | tf_op jit(solution)/shard_map/pallas_call | solution.py:373
  96.9 1.7 %copy.7 = bf16[1,192,8192]{2,1,0:T(8,128)(2,1)} copy(bf16[1,192,8192]{2,1,0:T(8,128)(2,1)S(1)} %shard_map.55) | data formatting | bytes 6291456
